TPU v7x, 32 devices: a whole 2x2x4 slice. The times are simulated.
32 devices in a mesh: leaf: 2 (over x), row: 4 (over y, core), col: 4 (over z).
Axes of the slice: x: 2, y: 2, z: 4, core: 2. Of those that a mesh axis runs over, the one named last changes fastest.
Arguments:
- leaf_front: float32 [2, 7, 4, 128, 7, 4, 128], P('leaf', None, 'row', None, None, 'col')
- leaf_pattern: int32 [2, 28, 28], P('leaf'), may hold values from 0 to 1, as said below
- parent_panel: float32 [1, 2, 7, 4, 128, 4, 128], P(None, 'leaf', None, 'row', None, 'col'), may hold values from -0.125 to 0.125
- parent_diag: float32 [1, 2, 7, 4, 128], P(None, 'leaf', None, 'row'), may hold values from 1.5 to 2.5
- parent_pattern: int32 [1, 2, 28, 28], replicated, may hold values from 0 to 1, as said below
- ext_map: int32 [1, 2, 24], replicated, may hold values from 0 to 27, as said below
Outputs:
- panels: float32 [2, 2, 7, 4, 128, 4, 128], P(None, 'leaf', None, 'row', None, 'col')
- top_update: float32 [2, 6, 4, 128, 6, 4, 128], P('leaf', None, 'row', None, None, 'col')
Inputs may be any that keep to these rules, and one draw needn't show every extreme that they name: leaf_pattern: symmetric, with every diagonal block 1. parent_pattern: symmetric, with every diagonal block 1. parent_pattern[d, n] belongs to node n at depth d+1; rows n of 2 / 2^(d+1) or more are not read. ext_map[d, n] belongs to node n at depth d; rows n of 2 / 2^d or more are not read. Along its 24 entries it rises strictly; ext_map[d, n, j] - j is the same for the 4 entries j of each aligned run of 4, never falls and lies in 0 to 4. Among the entries j of one class of j mod 4, at most two lie in one class of ext_map mod 4, and in every row some two do.
All inputs are finite; a program needn't handle non-finite values.
Results may differ from a plain program's by a relative error of at most 0.0003.
Values sent between devices are 32-bit elements; how exact they have to be, the bound alone decides.
A program may use at most 128 MiB of HBM per device.

v0:
```python
import functools
import jax
import jax.numpy as jnp
from jax import lax
from jax.experimental import pallas as pl
from jax.experimental.pallas import tpu as pltpu
from jax.sharding import PartitionSpec as P

highest = lax.Precision.HIGHEST
MESH = pl.DeviceIdType.MESH
f32 = jnp.float32
bf16 = jnp.bfloat16


def symmetric_lower(matrix):
    size = matrix.shape[0]
    row = lax.broadcasted_iota(jnp.int32, (size, size), 0)
    col = lax.broadcasted_iota(jnp.int32, (size, size), 1)
    return jnp.where(row >= col, matrix, matrix.T)


def eliminate_block(block):
    size = block.shape[0]
    groups = size // 8
    lane = lax.broadcasted_iota(jnp.int32, (8, size), 1)
    sub = lax.broadcasted_iota(jnp.int32, (8, size), 0)
    rows = [block[8 * g : 8 * g + 8, :] for g in range(groups)]
    for g in range(groups):
        base = 8 * g
        here = rows[g]
        inside = jnp.logical_and(lane >= base, lane < base + 8)
        line = [jnp.broadcast_to(here[a : a + 1, :], (8, size)) for a in range(8)]
        s = [
            [
                jnp.broadcast_to(line[a][:, base + b : base + b + 1], (8, size)) if b >= a else None
                for b in range(8)
            ]
            for a in range(8)
        ]
        line = [
            jnp.where(inside, jnp.where(lane == base + a, 1.0, 0.0), line[a]) for a in range(8)
        ]
        inverse = [None] * 8
        ratio = [[None] * 8 for _ in range(8)]
        for a in range(8):
            inverse[a] = 1.0 / s[a][a]
            for b in range(a + 1, 8):
                ratio[a][b] = s[a][b] * inverse[a]
            for b in range(a + 1, 8):
                for c in range(b, 8):
                    s[b][c] = s[b][c] - ratio[a][b] * s[a][c]
                line[b] = line[b] - ratio[a][b] * line[a]
        done = line[0]
        for a in range(8):
            whole = line[a]
            for b in range(a, 8):
                whole = jnp.where(lane == base + b, s[a][b], whole)
            done = whole if a == 0 else jnp.where(sub == a, whole, done)
        rows[g] = done
        if g + 1 < groups:
            solved = [None] * 8
            for a in range(7, -1, -1):
                total = line[a] * inverse[a]
                for b in range(a + 1, 8):
                    total = total - ratio[a][b] * solved[b]
                solved[a] = total
            for h in range(g + 1, groups):
                before = rows[h]
                total = jnp.where(inside, 0.0, before)
                for a in range(8):
                    spread = jnp.broadcast_to(before[:, base + a : base + a + 1], (8, size))
                    total = total - spread * solved[a]
                rows[h] = total
    return jnp.concatenate(rows, axis=0)


def pivot_step(start, block_size, inverse_ref, upper_ref, row_ref):
    order = inverse_ref.shape[0]
    row_id = lax.broadcasted_iota(jnp.int32, (block_size, block_size), 0)
    col_id = lax.broadcasted_iota(jnp.int32, (block_size, block_size), 1)
    wide_col = lax.broadcasted_iota(jnp.int32, (block_size, order), 1)
    tall_row = lax.broadcasted_iota(jnp.int32, (order, block_size), 0)
    here = pl.ds(start, block_size)
    reduced = eliminate_block(inverse_ref[here, here])
    pivot = jnp.sum(jnp.where(row_id == col_id, reduced, 0.0), axis=1, keepdims=True)
    scale = lax.rsqrt(pivot)
    scale = scale * (1.5 - 0.5 * pivot * scale * scale)
    scaled = reduced * scale
    small = jnp.where(row_id > col_id, scaled, jnp.where(row_id == col_id, scale, 0.0))
    row = jnp.dot(small, inverse_ref[here, :], precision=highest, preferred_element_type=f32)
    right = jnp.where(wide_col >= start + block_size, row, 0.0)
    upper_ref[here, :] = right
    upper_ref[here, here] = jnp.where(row_id <= col_id, scaled, 0.0)
    row_ref[...] = row
    row_ref[:, here] = small
    inverse_ref[:, here] = jnp.where(tall_row >= start + block_size, 0.0, inverse_ref[:, here])
    inverse_ref[...] = inverse_ref[...] - lax.dot_general(
        right,
        row_ref[...],
        (((0,), (0,)), ((), ())),
        precision=highest,
        preferred_element_type=f32,
    )
    inverse_ref[here, :] = jnp.where(wide_col < start + block_size, row_ref[...], 0.0)


def split(value):
    high = value.astype(bf16)
    return high, (value - high.astype(f32)).astype(bf16)


def product(left, right):
    dims = (((1,), (1,)), ((), ()))
    pairs = ((left[1], right[0]), (left[0], right[1]), (left[0], right[0]))
    parts = [lax.dot_general(a, b, dims, preferred_element_type=f32) for a, b in pairs]
    return (parts[0] + parts[1]) + parts[2]


def run(when, act):
    if when is True:
        act()
    else:
        pl.when(when)(act)


class Group:
    def __init__(self, side, rows, size, wide, sems):
        self.side, self.rows, self.size, self.wide = side, rows, size, wide
        self.p = lax.axis_index("row")
        self.q = lax.axis_index("col")
        self.core = self.p + 1 - 2 * lax.rem(self.p, 2)
        self.far = lax.rem(self.p + side // 2, side)
        self.diagonal = lax.rem(self.core + side // 2, side)
        self.sems = sems
        self.sent = []

    def columns(self, source):
        return pl.ds(pl.multiple_of(source * self.size, self.size), self.size)

    def copy(self, source, target, send, receive, place):
        return pltpu.make_async_remote_copy(
            src_ref=source,
            dst_ref=target,
            send_sem=send,
            recv_sem=receive,
            device_id=place,
            device_id_type=MESH,
        )

    def start(self, when, make):
        run(when, lambda: make().start())
        self.sent.append((when, make))

    def finish(self):
        for when, make in self.sent:
            run(when, lambda: make().wait_send())
        self.sent = []

    def spot(self, row, source, part):
        if part == "corner":
            return self.wide.at[row, 0, :, self.columns(source)]
        return self.wide.at[row, 1 : self.rows, :, self.columns(source)]

    def strip(self, row):
        return self.wide.at[row, 0]


def gather_corner(group, column):
    p, q, side = group.p, group.q, group.side
    z_send, z_recv, s_send, s_recv = group.sems[:4]
    group.wide[p, 0, :, group.columns(q)] = column[0]
    for hop in range(1, side):
        to = lax.rem(q + hop, side)

        def make(to=to, hop=hop):
            return group.copy(
                column.at[0],
                group.spot(p, q, "corner"),
                z_send.at[hop],
                z_recv.at[q],
                {"col": to},
            )

        group.start(True, make)


def gather_strips(group):
    p, q, side = group.p, group.q, group.side
    z_send, z_recv, s_send, s_recv = group.sems[:4]
    for hop in range(1, side):
        source = lax.rem(q + hop, side)
        spot = group.spot(p, source, "corner")
        group.copy(spot, spot, z_send.at[0], z_recv.at[source], {"col": q}).wait_recv()
    for index, place in ((0, group.core), (1, group.far)):

        def make(index=index, place=place):
            return group.copy(
                group.strip(p), group.strip(p), s_send.at[index], s_recv.at[index], {"row": place}
            )

        group.start(True, make)

    def wait(index, row):
        group.copy(
            group.strip(row), group.strip(row), s_send.at[index], s_recv.at[index], {"row": p}
        ).wait_recv()

    wait(1, group.far)

    def make():
        return group.copy(
            group.strip(group.far),
            group.strip(group.far),
            s_send.at[2],
            s_recv.at[2],
            {"row": group.core},
        )

    group.start(True, make)
    wait(0, group.core)
    wait(2, group.diagonal)


def load_corner(group, inverse_ref):
    side, size = group.side, group.size
    for row in range(side):
        for col in range(row + 1):
            block = group.wide[row, 0, :, col * size : (col + 1) * size]
            if row == col:
                inverse_ref[row * size : (row + 1) * size, col * size : (col + 1) * size] = (
                    symmetric_lower(block)
                )
            else:
                inverse_ref[row * size : (row + 1) * size, col * size : (col + 1) * size] = block
                inverse_ref[col * size : (col + 1) * size, row * size : (row + 1) * size] = block.T


class Lines:
    def __init__(self, group, column, every):
        self.group, self.column, self.every = group, column, every

    def wanted(self, row):
        return True if self.every else row == self.group.q

    def both(self, *conditions):
        kept = [c for c in conditions if c is not True]
        return functools.reduce(jnp.logical_and, kept) if kept else True

    def inside(self, source):
        return jnp.logical_and(source >= 0, source < self.group.side)

    def hop(self, step, act):
        g = self.group
        send, receive = g.sems[4:6]
        for index, sign in ((0, 1), (1, -1)):
            source = g.q - sign * (step - 1)
            to = g.q + sign

            def make(index=index, source=source, to=to):
                spot = g.spot(g.p, source, "lines")
                return g.copy(
                    spot, spot, send.at[2 * (step - 1) + index], receive.at[source], {"col": to}
                )

            when = jnp.logical_and(self.inside(source), self.inside(to))
            run(when, lambda: act(make()))

    def arrive(self, step):
        g = self.group
        send, receive = g.sems[4:6]
        for sign in (1, -1):
            source = g.q - sign * step

            def wait(source=source):
                spot = g.spot(g.p, source, "lines")
                g.copy(spot, spot, send.at[0], receive.at[source], {"col": g.q}).wait_recv()

            run(self.inside(source), wait)

    def sources(self, step):
        out = []
        for sign in (1, -1):
            source = self.group.q - sign * step
            valid = self.inside(source)
            if sign < 0:
                valid = jnp.logical_and(valid, step > 0)
            out.append((valid, source))
        return out

    def across(self, step, act):
        g = self.group
        send, receive = g.sems[6:8]
        for valid, source in self.sources(step):
            for index, place in ((0, g.far), (1, g.core)):

                def make(index=index, place=place, source=source):
                    spot = g.spot(g.p, source, "lines")
                    return g.copy(
                        spot,
                        spot,
                        send.at[index, source],
                        receive.at[index, source],
                        {"row": place},
                    )

                run(self.both(valid, self.wanted(g.p)), lambda: act(make()))

    def pass_on(self, step, act, first):
        g = self.group
        send, receive = g.sems[6:8]
        for valid, source in self.sources(step):

            def make(source=source):
                spot = g.spot(g.far, source, "lines")
                return g.copy(
                    spot, spot, send.at[2, source], receive.at[2, source], {"row": g.core}
                )

            def whole(source=source, make=make):
                if first:
                    spot = g.spot(g.far, source, "lines")
                    g.copy(
                        spot, spot, send.at[0, source], receive.at[0, source], {"row": g.p}
                    ).wait_recv()
                act(make())

            run(self.both(valid, self.wanted(g.far)), whole)

    def last(self):
        g = self.group
        send, receive = g.sems[6:8]
        for index, row in ((1, g.core), (2, g.diagonal)):
            for source in range(g.side):

                def wait(index=index, row=row, source=source):
                    spot = g.spot(row, source, "lines")
                    g.copy(
                        spot,
                        spot,
                        send.at[index, source],
                        receive.at[index, source],
                        {"row": g.p},
                    ).wait_recv()

                run(self.wanted(row), wait)

    def open(self):
        self.hop(1, begin)
        self.across(0, begin)

    def advance(self, step):
        side = self.group.side

        @pl.when(step + 1 < side)
        def _():
            self.arrive(step + 1)

            @pl.when(step + 2 < side)
            def _():
                self.hop(step + 2, begin)

            self.across(step + 1, begin)

        self.pass_on(step, begin, True)

    def finish(self):
        def body(step, carry):
            pl.when(step > 0)(lambda: self.hop(step, settle))
            self.across(step, settle)
            self.pass_on(step, settle, False)
            return carry

        lax.fori_loop(0, self.group.side, body, 0)


def begin(copy):
    copy.start()


def settle(copy):
    copy.wait_send()


def gather_sems(side):
    return [
        pltpu.SemaphoreType.DMA((side,)),
        pltpu.SemaphoreType.DMA((side,)),
        pltpu.SemaphoreType.DMA((3,)),
        pltpu.SemaphoreType.DMA((3,)),
        pltpu.SemaphoreType.DMA((2 * side,)),
        pltpu.SemaphoreType.DMA((side,)),
        pltpu.SemaphoreType.DMA((3, side)),
        pltpu.SemaphoreType.DMA((3, side)),
    ]


def meet(places):
    barrier = pltpu.get_barrier_semaphore()
    for place in places:
        pl.semaphore_signal(barrier, inc=1, device_id=place, device_id_type=MESH)
    pl.semaphore_wait(barrier, len(places))


def top_block(upper_ref, p, q, size):
    block = upper_ref[
        pl.ds(pl.multiple_of(q * size, size), size), pl.ds(pl.multiple_of(p * size, size), size)
    ]
    return jnp.where(p >= q, block.T, 0.0)


def tri(row, col, rows):
    return col * rows - col * (col - 1) // 2 + row - col


def factor(group, lines, inverse, upper, row_ref, extra):
    size = group.size

    def body(step, carry):
        pivot_step(pl.multiple_of(step * size, size), size, inverse, upper, row_ref)
        lines.advance(step)
        extra(step)
        return carry

    lax.fori_loop(0, group.side, body, 0)


def child_kernel(
    packed,
    node,
    map_ref,
    mask_ref,
    above_ref,
    front,
    share_ref,
    diag_ref,
    panel_ref,
    part_ref,
    column,
    inner,
    pack,
    recv,
    wide,
    inverse,
    upper,
    row_ref,
    inv_hi,
    inv_lo,
    tall,
    l_hi,
    l_lo,
    load_sem,
    f_send,
    f_recv,
    *sems,
):
    child, parent = node
    rows, size = column.shape[0], column.shape[1]
    runs = rows - 1
    side = wide.shape[0]
    group = Group(side, rows, size, wide, sems)
    p, q = group.p, group.q

    def block_of(t, u):
        if packed:
            return front.at[tri(t, u, rows)]
        return front.at[0, t, 0, :, u, 0, :]

    def place_of(t, u):
        return column.at[t] if u == 0 else inner.at[(t - 1) * runs + u - 1]

    spots = [(t, u) for u in range(rows) for t in range(u, rows)]
    loads = [
        pltpu.make_async_copy(block_of(t, u), place_of(t, u), load_sem.at[index])
        for index, (t, u) in enumerate(spots)
    ]
    for load in loads:
        load.start()
    others = []
    for r in range(side):
        for c in range(side):
            if r or c:
                others.append({"row": lax.rem(p + r, side), "col": lax.rem(q + c, side)})
    meet(others)

    def masked(t, u):
        if packed:
            return 1.0
        return mask_ref[side * t + p, side * u + q].astype(f32)

    loads[0].wait()
    column[0] = column[0] * masked(0, 0)
    gather_corner(group, column)
    for t in range(1, rows):
        loads[t].wait()
        column[t] = column[t] * masked(t, 0)
    wide[p, 1:rows, :, group.columns(q)] = column[1:rows]
    lines = Lines(group, column, True)
    lines.open()
    for index in range(rows, len(spots)):
        loads[index].wait()

    shift = [jnp.clip(map_ref[child, side * k] - side * k, 0, side) for k in range(runs)]
    kind = [lax.rem(s, side) for s in shift]
    rank = []
    for k in range(runs):
        count = jnp.int32(0)
        for j in range(k):
            count = count + jnp.where(kind[j] == kind[k], 1, 0)
        rank.append(jnp.minimum(count, 1))
    chosen = []
    for r in range(side):
        pair = []
        for i in range(2):
            found = jnp.int32(0)
            for k in range(runs):
                hit = jnp.logical_and(kind[k] == r, rank[k] == i)
                found = jnp.where(hit, k, found)
            pair.append(found)
        chosen.append(pair)

    def slots_of(r, c):
        if r == c:
            return [(0, 0), (1, 0), (1, 1)]
        if 1 <= r < c:
            return []
        return [(0, 0), (0, 1), (1, 0), (1, 1)]

    moves = []
    for c in range(side):
        for r in range(side):
            slots = slots_of(r, c)
            if not slots:
                continue
            for slot, (i, j) in enumerate(slots):
                k, l = chosen[r][i], chosen[c][j]
                k, l = jnp.maximum(k, l), jnp.minimum(k, l)
                block = inner[k * runs + l]
                if not packed:
                    block = block * mask_ref[side * (k + 1) + p, side * (l + 1) + q].astype(f32)
                if r or c:
                    pack[r * side + c, slot] = block
                else:
                    recv[0, slot] = block
            if r or c:
                moves.append((r, c, len(slots)))

    def move(r, c, count):
        index = r * side + c
        return lambda: group.copy(
            pack.at[index, 0:count],
            recv.at[index, 0:count],
            f_send.at[index],
            f_recv.at[index],
            {"row": lax.rem(p + r, side), "col": lax.rem(q + c, side)},
        )

    gather_strips(group)
    load_corner(group, inverse)
    order = sorted(moves, key=lambda m: -min(m[1], side - m[1]))
    per = -(-len(order) // (side - 1))

    def extra(step):
        for turn in range(side - 1):

            @pl.when(step == turn)
            def _():
                for r, c, count in order[turn * per : (turn + 1) * per]:
                    move(r, c, count)().start()

    factor(group, lines, inverse, upper, row_ref, extra)
    lines.last()
    inv_hi[...], inv_lo[...] = split(inverse[...])

    def home(spot, mine):
        row_k = row_ps = ok = kinds = ranks = jnp.int32(0)
        for k in range(runs):
            ps = side * spot + mine - shift[k] - side * k
            valid = jnp.logical_and(ps >= 0, ps < side)
            row_k, row_ps = jnp.where(valid, k, row_k), jnp.where(valid, ps, row_ps)
            kinds, ranks = jnp.where(valid, kind[k], kinds), jnp.where(valid, rank[k], ranks)
            ok = jnp.where(valid, 1, ok)
        return row_k, row_ps, ok, kinds, ranks

    row_home = [home(t, p) for t in range(rows)]
    col_home = [home(t, q) for t in range(rows)]
    for index, (k, ps, ok, _, _) in enumerate(row_home + col_home):
        block = wide[ps, k + 1]
        tall[index // 2, (index % 2) * size : (index % 2 + 1) * size, :] = jnp.where(
            ok > 0, block, 0.0
        )

    def times(index, carry):
        value = product(split(tall[index]), (inv_hi[...], inv_lo[...]))
        at = pl.ds(pl.multiple_of(index * 2 * size, 2 * size), 2 * size)
        l_hi[at, :], l_lo[at, :] = split(value)
        return carry

    lax.fori_loop(0, rows, times, 0)
    own = pl.ds(pl.multiple_of(q * size, size), size)
    panel_ref[0] = top_block(upper, p, q, size)
    left = wide[p, 1:rows].reshape(runs * size, side * size)
    below = product(split(left), (inv_hi[own, :], inv_lo[own, :]))
    panel_ref[1:rows] = below.reshape(runs, size, size)

    for r, c, count in order:
        move(r, c, count)().wait()
    high = rows * size
    row_id = lax.broadcasted_iota(jnp.int32, (size, size), 0)
    col_id = lax.broadcasted_iota(jnp.int32, (size, size), 1)
    ranges = [(0, 1)] + [(u, min(u + 2, rows)) for u in range(1, rows, 2)]
    for first, end in ranges:
        taken = slice(first * size, high)
        given = slice(high + first * size, high + end * size)
        out = product((l_hi[taken, :], l_lo[taken, :]), (l_hi[given, :], l_lo[given, :]))
        for u in range(first, end):
            _, _, c_ok, c_kind, c_rank = col_home[u]
            for t in range(u, rows):
                _, _, r_ok, r_kind, r_rank = row_home[t]
                slot = jnp.where(r_kind == c_kind, r_rank + c_rank, 2 * r_rank + c_rank)
                block = recv[r_kind * side + c_kind, slot]
                value = jnp.where(r_ok * c_ok > 0, block, 0.0)
                value = value - out[
                    (t - first) * size : (t - first + 1) * size,
                    (u - first) * size : (u - first + 1) * size,
                ]
                if u == 0:
                    value = value + share_ref[t] * above_ref[parent, side * t + p, q].astype(f32)
                if t == u:
                    factor_here = above_ref[parent, side * t + p, side * t + q].astype(f32)
                    on = jnp.logical_and(row_id == col_id, p == q)
                    value = value + jnp.where(on, diag_ref[t] * factor_here, 0.0)
                part_ref[tri(t, u, rows)] = value
    lines.finish()
    group.finish()


def params(name, key):
    return dict(
        name=name,
        compiler_params=pltpu.CompilerParams(
            collective_id=key, has_side_effects=True, vmem_limit_bytes=60 * 2**20
        ),
    )


VM = pl.BlockSpec(memory_space=pltpu.VMEM)
SM = pl.BlockSpec(memory_space=pltpu.SMEM)
ANY = pl.BlockSpec(memory_space=pl.ANY)


def run_child(key, packed, child, parent, maps, mask, above, front, share, diag, side):
    rows, size = share.shape[0], share.shape[1]
    runs = rows - 1
    order = side * size
    lower = rows * (rows + 1) // 2
    VMEM, DMA = pltpu.VMEM, pltpu.SemaphoreType.DMA

    def body(*refs):
        leaf = lax.axis_index("leaf")
        child_kernel(packed, (leaf // child, leaf // parent), *refs)

    return pl.pallas_call(
        body,
        out_shape=(
            jax.ShapeDtypeStruct((rows, size, size), f32),
            jax.ShapeDtypeStruct((lower, size, size), f32),
        ),
        in_specs=[SM, SM, SM, ANY, VM, VM],
        out_specs=(VM, VM),
        scratch_shapes=[
            VMEM((rows, size, size), f32),
            VMEM((runs * runs, size, size), f32),
            VMEM((side * side, 4, size, size), f32),
            VMEM((side * side, 4, size, size), f32),
            VMEM((side, rows, size, order), f32),
            VMEM((order, order), f32),
            VMEM((order, order), f32),
            VMEM((size, order), f32),
            VMEM((order, order), bf16),
            VMEM((order, order), bf16),
            VMEM((rows, 2 * size, order), f32),
            VMEM((2 * rows * size, order), bf16),
            VMEM((2 * rows * size, order), bf16),
            DMA((lower,)),
            DMA((side * side,)),
            DMA((side * side,)),
            *gather_sems(side),
        ],
        **params(f"child_{key}", key),
    )(maps, mask, above, front, share, diag)


def top_kernel(
    bit,
    mine,
    early,
    panels_ref,
    top_ref,
    theirs,
    column,
    wide,
    inverse,
    upper,
    row_ref,
    inv_hi,
    inv_lo,
    l_hi,
    l_lo,
    done,
    blank,
    x_send,
    x_recv,
    out_sem,
    *sems,
):
    rows, size = column.shape[0], column.shape[1]
    runs = rows - 1
    side = wide.shape[0]
    group = Group(side, rows, size, wide, sems)
    p, q = group.p, group.q
    leaf = lax.axis_index("leaf")
    partner = leaf + bit - 2 * bit * lax.rem(leaf // bit, 2)
    places = [{"leaf": partner}, {"row": group.core}, {"row": group.far}]
    for hop in range(1, side):
        places.append({"col": lax.rem(q + hop, side)})
    meet(places)
    lower = mine.shape[0]
    cuts = [(0, 1), (1, rows), (rows, lower)]

    def trade(index):
        low, high = cuts[index]
        return lambda: group.copy(
            mine.at[low:high],
            theirs.at[low:high],
            x_send.at[index],
            x_recv.at[index],
            {"leaf": partner},
        )

    for index in range(len(cuts)):
        group.start(True, trade(index))
    blank[...] = jnp.zeros_like(blank)
    for k in range(panels_ref.shape[0] - 1):
        panels_ref[k] = early[k]
    trade(0)().wait_recv()
    column[0] = mine[0] + theirs[0]
    gather_corner(group, column)
    trade(1)().wait_recv()
    for t in range(1, rows):
        column[t] = mine[t] + theirs[t]
    wide[p, 1:rows, :, group.columns(q)] = column[1:rows]
    lines = Lines(group, column, False)
    lines.open()
    gather_strips(group)
    load_corner(group, inverse)
    factor(group, lines, inverse, upper, row_ref, lambda step: None)
    lines.last()
    inv_hi[...], inv_lo[...] = split(inverse[...])
    last = panels_ref.shape[0] - 1
    panels_ref[last, 0] = top_block(upper, p, q, size)
    own = pl.ds(pl.multiple_of(q * size, size), size)

    def times(index, carry):
        row = jnp.where(index < runs, p, q)
        t = jnp.where(index < runs, index, index - runs) + 1
        value = product(split(wide[row, t]), (inv_hi[...], inv_lo[...]))
        at = pl.ds(pl.multiple_of(index * size, size), size)
        l_hi[at, :], l_lo[at, :] = split(value)
        return carry

    lax.fori_loop(0, 2 * runs, times, 0)
    left = wide[p, 1:rows].reshape(runs * size, side * size)
    below = product(split(left), (inv_hi[own, :], inv_lo[own, :]))
    panels_ref[last, 1:rows] = below.reshape(runs, size, size)
    trade(2)().wait_recv()
    high = runs * size
    row_id = lax.broadcasted_iota(jnp.int32, (size, size), 0)
    col_id = lax.broadcasted_iota(jnp.int32, (size, size), 1)
    writes = []
    for k in range(runs):
        for l in range(runs):
            source = blank if k < l else done.at[k * runs + l]
            writes.append(
                pltpu.make_async_copy(
                    source, top_ref.at[0, k, 0, :, l, 0, :], out_sem.at[k * runs + l]
                )
            )
            if k < l:
                writes[-1].start()
    for first in range(0, runs, 2):
        end = min(first + 2, runs)
        taken = slice(first * size, high)
        given = slice(high + first * size, high + end * size)
        out = product((l_hi[taken, :], l_lo[taken, :]), (l_hi[given, :], l_lo[given, :]))
        for l in range(first, end):
            for k in range(l, runs):
                at = tri(k + 1, l + 1, rows)
                value = (mine[at] + theirs[at]) - out[
                    (k - first) * size : (k - first + 1) * size,
                    (l - first) * size : (l - first + 1) * size,
                ]
                if k == l:
                    keep = jnp.logical_or(p > q, jnp.logical_and(p == q, row_id >= col_id))
                    value = jnp.where(keep, value, 0.0)
                done[k * runs + l] = value
                writes[k * runs + l].start()
    for write in writes:
        write.wait()
    lines.finish()
    group.finish()


def run_top(key, bit, part, early, rows, side):
    size = part.shape[1]
    runs = rows - 1
    order = side * size
    VMEM, DMA = pltpu.VMEM, pltpu.SemaphoreType.DMA
    return pl.pallas_call(
        functools.partial(top_kernel, bit),
        out_shape=(
            jax.ShapeDtypeStruct((early.shape[0] + 1, rows, size, size), f32),
            jax.ShapeDtypeStruct((1, runs, 1, size, runs, 1, size), f32),
        ),
        in_specs=[VM, VM],
        out_specs=(VM, ANY),
        scratch_shapes=[
            VMEM(part.shape, f32),
            VMEM((rows, size, size), f32),
            VMEM((side, rows, size, order), f32),
            VMEM((order, order), f32),
            VMEM((order, order), f32),
            VMEM((size, order), f32),
            VMEM((order, order), bf16),
            VMEM((order, order), bf16),
            VMEM((2 * runs * size, order), bf16),
            VMEM((2 * runs * size, order), bf16),
            VMEM((runs * runs, size, size), f32),
            VMEM((size, size), f32),
            DMA((3,)),
            DMA((3,)),
            DMA((runs * runs,)),
            *gather_sems(side),
        ],
        **params(f"top_{key}", key),
    )(part, early)


def partner_2(block, axis, bit):
    count = lax.axis_size(axis)
    route = []
    for low in range(count):
        high = low | 1 << bit
        if high != low and high < count:
            route += [(low, high), (high, low)]
    return lax.ppermute(block, axis, route)


def shards(leaf_front, leaf_pattern, parent_panel, parent_diag, parent_pattern, ext_map):
    rows = leaf_front.shape[1]
    size = leaf_front.shape[3]
    levels = parent_panel.shape[0]
    side = lax.axis_size("row")
    share = parent_panel.reshape(levels, rows, size, size)
    diag = parent_diag.reshape(levels, rows, 1, size)
    front, packed = leaf_front, False
    panel_list = []
    for depth in range(levels):
        panel, part = run_child(
            depth,
            packed,
            1 << depth,
            2 << depth,
            ext_map[depth],
            leaf_pattern[0],
            parent_pattern[depth],
            front,
            share[depth],
            diag[depth],
            side,
        )
        panel_list.append(panel)
        if depth + 1 < levels:
            front = part + partner_2(part, "leaf", depth)
            packed = True
            higher = (share[depth + 1 :], diag[depth + 1 :])
            other = partner_2(higher, "leaf", depth)
            share = jnp.concatenate([share[: depth + 1], higher[0] + other[0]], axis=0)
            diag = jnp.concatenate([diag[: depth + 1], higher[1] + other[1]], axis=0)
    panels, top_update = run_top(
        levels, 1 << (levels - 1), part, jnp.stack(panel_list), rows, side
    )
    return (panels.reshape(levels + 1, 1, rows, 1, size, 1, size), top_update)


def solution(mesh):
    return jax.shard_map(
        shards,
        mesh=mesh,
        in_specs=(
            P("leaf", None, "row", None, None, "col", None),
            P("leaf", None, None),
            P(None, "leaf", None, "row", None, "col", None),
            P(None, "leaf", None, "row", None),
            P(),
            P(),
        ),
        out_specs=(
            P(None, "leaf", None, "row", None, "col", None),
            P("leaf", None, "row", None, None, "col", None),
        ),
        check_vma=False,
    )
```

profile of v0, /device:TPU:0, one launch (start us, length us, event | category | flops | bytes accessed | tf_op | source)
XLA Modules:
  0.0 218.1 jit_solution(14169642431254138896)
XLA Ops:
  0.6 1.3 copy.14
  1.9 1.4 copy.13
  3.3 129.6 %child_0.1 = (f32[7,128,128]{2,1,0:T(8,128)}, f32[28,128,128]{2,1,0:T(8,128)}) custom-call(s32[2,24]{1,0:T(2,128)} %bitcast.19, s32[28,28]{1,0:T(8,128)} %bitcast.17, s32[2,28,28]{2,1,0:T(8,128)} %bitcast.16, f32[1,7,1,128,7,1,128]{6,5,4,3,2,1,0:T(1,128)} %refs_3_.1, f32[7,128,128]{2,1,0:T(8,128)} %bitcast.14, f32[7,1,128]{2,1,0:T(1,128)} %bitcast.18), custom_call_target="tpu_custom_call" | custom-call | tf_op jit(solution)/shard_map/child_0/pallas_call | solution.py:662
  132.9 78.3 %top_1.1 = (f32[2,7,128,128]{3,2,1,0:T(8,128)}, f32[1,6,1,128,6,1,128]{6,5,4,3,2,1,0:T(1,128)}) custom-call(f32[28,128,128]{2,1,0:T(8,128)} %get-tuple-element.6.mine, f32[1,7,128,128]{3,2,1,0:T(8,128)} %bitcast.15), custom_call_target="tpu_custom_call" | custom-call | tf_op jit(solution)/shard_map/top_1/pallas_call | solution.py:818
  211.3 2.2 copy.17
  213.5 4.7 %copy.18 = f32[1,6,1,128,6,1,128]{6,5,4,3,2,1,0:T(1,128)} copy(f32[1,6,1,128,6,1,128]{6,5,4,3,2,1,0:T(1,128)} %get-tuple-element.15) | data formatting | bytes 4718592
where the time goes:
time: 219 us; the launch traced here: 218 us
  Pallas kernels  208 us (95%)
  local copies, waits for them, and re-layouts  9.55 us (4%)
    pallas_call x1, Pallas kernels, run_child(): pl.pallas_call(body, out_shape=(jax.ShapeDtypeStruct((rows, size, size),...  130 us
    pallas_call x1, Pallas kernels, run_top(): pl.pallas_call(functools.partial(top_kernel, bit), out_shape=(jax.ShapeDt...  78.3 us
    unnamed x4, local copies, waits for them, and re-layouts  9.55 us

commit v1 on v0

--- a/solution.py
+++ b/solution.py
@@ -74,34 +74,28 @@
     return jnp.concatenate(rows, axis=0)
 
 
-def pivot_step(start, block_size, inverse_ref, upper_ref, row_ref):
-    order = inverse_ref.shape[0]
-    row_id = lax.broadcasted_iota(jnp.int32, (block_size, block_size), 0)
-    col_id = lax.broadcasted_iota(jnp.int32, (block_size, block_size), 1)
-    wide_col = lax.broadcasted_iota(jnp.int32, (block_size, order), 1)
-    tall_row = lax.broadcasted_iota(jnp.int32, (order, block_size), 0)
-    here = pl.ds(start, block_size)
-    reduced = eliminate_block(inverse_ref[here, here])
+def pivot_step(step, size, row_of, work):
+    row_ref, upper_ref, hi, lo = work
+    order = hi.shape[0]
+    start = pl.multiple_of(step * size, size)
+    here = pl.ds(start, size)
+    row_id = lax.broadcasted_iota(jnp.int32, (size, size), 0)
+    col_id = lax.broadcasted_iota(jnp.int32, (size, size), 1)
+    row_ref[...] = row_of(step) - three((hi[:, here], lo[:, here]), (hi[...], lo[...]), 0, 0)
+    hi[:, here] = jnp.zeros((order, size), bf16)
+    lo[:, here] = jnp.zeros((order, size), bf16)
+    reduced = eliminate_block(row_ref[:, here])
     pivot = jnp.sum(jnp.where(row_id == col_id, reduced, 0.0), axis=1, keepdims=True)
     scale = lax.rsqrt(pivot)
     scale = scale * (1.5 - 0.5 * pivot * scale * scale)
     scaled = reduced * scale
     small = jnp.where(row_id > col_id, scaled, jnp.where(row_id == col_id, scale, 0.0))
-    row = jnp.dot(small, inverse_ref[here, :], precision=highest, preferred_element_type=f32)
-    right = jnp.where(wide_col >= start + block_size, row, 0.0)
-    upper_ref[here, :] = right
+    row_ref[...] = three(split(small), split(row_ref[...]), 1, 0)
+    row_ref[:, here] = small
+    row = row_ref[...]
+    upper_ref[here, :] = row
     upper_ref[here, here] = jnp.where(row_id <= col_id, scaled, 0.0)
-    row_ref[...] = row
-    row_ref[:, here] = small
-    inverse_ref[:, here] = jnp.where(tall_row >= start + block_size, 0.0, inverse_ref[:, here])
-    inverse_ref[...] = inverse_ref[...] - lax.dot_general(
-        right,
-        row_ref[...],
-        (((0,), (0,)), ((), ())),
-        precision=highest,
-        preferred_element_type=f32,
-    )
-    inverse_ref[here, :] = jnp.where(wide_col < start + block_size, row_ref[...], 0.0)
+    hi[here, :], lo[here, :] = split(row)
 
 
 def split(value):
@@ -109,11 +103,15 @@
     return high, (value - high.astype(f32)).astype(bf16)
 
 
-def product(left, right):
-    dims = (((1,), (1,)), ((), ()))
+def three(left, right, left_dim, right_dim):
+    dims = (((left_dim,), (right_dim,)), ((), ()))
     pairs = ((left[1], right[0]), (left[0], right[1]), (left[0], right[0]))
     parts = [lax.dot_general(a, b, dims, preferred_element_type=f32) for a, b in pairs]
     return (parts[0] + parts[1]) + parts[2]
+
+
+def product(left, right):
+    return three(left, right, 1, 1)
 
 
 def run(when, act):
@@ -161,78 +159,82 @@
             return self.wide.at[row, 0, :, self.columns(source)]
         return self.wide.at[row, 1 : self.rows, :, self.columns(source)]
 
-    def strip(self, row):
-        return self.wide.at[row, 0]
-
-
-def gather_corner(group, column):
-    p, q, side = group.p, group.q, group.side
-    z_send, z_recv, s_send, s_recv = group.sems[:4]
-    group.wide[p, 0, :, group.columns(q)] = column[0]
-    for hop in range(1, side):
-        to = lax.rem(q + hop, side)
-
-        def make(to=to, hop=hop):
-            return group.copy(
-                column.at[0],
-                group.spot(p, q, "corner"),
-                z_send.at[hop],
-                z_recv.at[q],
-                {"col": to},
+    def mates(self):
+        return ((0, self.core), (1, self.far), (2, self.diagonal))
+
+
+class Corner:
+    def __init__(self, group, column):
+        self.group, self.column = group, column
+
+    def along(self, act):
+        g = self.group
+        for hop in range(1, g.side):
+
+            def make(hop=hop):
+                return g.copy(
+                    self.column.at[0],
+                    g.spot(g.p, g.q, "corner"),
+                    g.sems[0].at[hop],
+                    g.sems[1].at[g.q],
+                    {"col": lax.rem(g.q + hop, g.side)},
+                )
+
+            run(g.p >= g.q, lambda: act(make()))
+
+    def piece(self, index, row, place, source):
+        g = self.group
+        spot = g.spot(row, source, "corner")
+        return g.copy(
+            spot, spot, g.sems[2].at[index, source], g.sems[3].at[index, source], {"row": place}
+        )
+
+    def open(self):
+        g = self.group
+        g.wide[g.p, 0, :, g.columns(g.q)] = self.column[0]
+        self.along(begin)
+
+    def spread(self):
+        g = self.group
+        for source in range(g.side):
+
+            def arrive(source=source):
+                spot = g.spot(g.p, source, "corner")
+                g.copy(
+                    spot, spot, g.sems[0].at[0], g.sems[1].at[source], {"col": g.q}
+                ).wait_recv()
+
+            run(jnp.logical_and(g.p >= source, g.q != source), arrive)
+            self.across(source, begin)
+
+    def across(self, source, act):
+        g = self.group
+
+        def body():
+            for index, place in g.mates():
+                act(self.piece(index, g.p, place, source))
+
+        run(g.p >= source, body)
+
+    def need(self, step):
+        g = self.group
+        for index, row in g.mates():
+            run(row >= step, lambda: self.piece(index, row, g.p, step).wait_recv())
+
+    def row(self, step):
+        g = self.group
+        blocks = []
+        for j in range(g.side):
+            block = g.wide[j, 0, :, g.columns(step)]
+            blocks.append(
+                jnp.where(j > step, block.T, jnp.where(j == step, symmetric_lower(block), 0.0))
             )
-
-        group.start(True, make)
-
-
-def gather_strips(group):
-    p, q, side = group.p, group.q, group.side
-    z_send, z_recv, s_send, s_recv = group.sems[:4]
-    for hop in range(1, side):
-        source = lax.rem(q + hop, side)
-        spot = group.spot(p, source, "corner")
-        group.copy(spot, spot, z_send.at[0], z_recv.at[source], {"col": q}).wait_recv()
-    for index, place in ((0, group.core), (1, group.far)):
-
-        def make(index=index, place=place):
-            return group.copy(
-                group.strip(p), group.strip(p), s_send.at[index], s_recv.at[index], {"row": place}
-            )
-
-        group.start(True, make)
-
-    def wait(index, row):
-        group.copy(
-            group.strip(row), group.strip(row), s_send.at[index], s_recv.at[index], {"row": p}
-        ).wait_recv()
-
-    wait(1, group.far)
-
-    def make():
-        return group.copy(
-            group.strip(group.far),
-            group.strip(group.far),
-            s_send.at[2],
-            s_recv.at[2],
-            {"row": group.core},
-        )
-
-    group.start(True, make)
-    wait(0, group.core)
-    wait(2, group.diagonal)
-
-
-def load_corner(group, inverse_ref):
-    side, size = group.side, group.size
-    for row in range(side):
-        for col in range(row + 1):
-            block = group.wide[row, 0, :, col * size : (col + 1) * size]
-            if row == col:
-                inverse_ref[row * size : (row + 1) * size, col * size : (col + 1) * size] = (
-                    symmetric_lower(block)
-                )
-            else:
-                inverse_ref[row * size : (row + 1) * size, col * size : (col + 1) * size] = block
-                inverse_ref[col * size : (col + 1) * size, row * size : (row + 1) * size] = block.T
+        return jnp.concatenate(blocks, axis=1)
+
+    def finish(self):
+        self.along(settle)
+        for source in range(self.group.side):
+            self.across(source, settle)
 
 
 class Lines:
@@ -385,8 +387,8 @@
     return [
         pltpu.SemaphoreType.DMA((side,)),
         pltpu.SemaphoreType.DMA((side,)),
-        pltpu.SemaphoreType.DMA((3,)),
-        pltpu.SemaphoreType.DMA((3,)),
+        pltpu.SemaphoreType.DMA((3, side)),
+        pltpu.SemaphoreType.DMA((3, side)),
         pltpu.SemaphoreType.DMA((2 * side,)),
         pltpu.SemaphoreType.DMA((side,)),
         pltpu.SemaphoreType.DMA((3, side)),
@@ -412,11 +414,14 @@
     return col * rows - col * (col - 1) // 2 + row - col
 
 
-def factor(group, lines, inverse, upper, row_ref, extra):
-    size = group.size
+def factor(group, corner, lines, work, extra):
+    hi, lo = work[2:]
+    hi[...] = jnp.zeros_like(hi)
+    lo[...] = jnp.zeros_like(lo)
 
     def body(step, carry):
-        pivot_step(pl.multiple_of(step * size, size), size, inverse, upper, row_ref)
+        corner.need(step)
+        pivot_step(step, group.size, corner.row, work)
         lines.advance(step)
         extra(step)
         return carry
@@ -424,40 +429,14 @@
     lax.fori_loop(0, group.side, body, 0)
 
 
-def child_kernel(
-    packed,
-    node,
-    map_ref,
-    mask_ref,
-    above_ref,
-    front,
-    share_ref,
-    diag_ref,
-    panel_ref,
-    part_ref,
-    column,
-    inner,
-    pack,
-    recv,
-    wide,
-    inverse,
-    upper,
-    row_ref,
-    inv_hi,
-    inv_lo,
-    tall,
-    l_hi,
-    l_lo,
-    load_sem,
-    f_send,
-    f_recv,
-    *sems,
-):
+def child_phase(packed, node, front_refs, part_ref, panel_ref, refs, sems, group):
+    map_ref, mask_ref, above_ref, front, share_ref, diag_ref = front_refs
+    (column, inner, pack, near, late, wide, row_ref, upper, hi, lo, tall, l_hi, l_lo, table) = refs
+    load_sem, n_send, n_recv, f_send, f_recv = sems
     child, parent = node
     rows, size = column.shape[0], column.shape[1]
     runs = rows - 1
     side = wide.shape[0]
-    group = Group(side, rows, size, wide, sems)
     p, q = group.p, group.q
 
     def block_of(t, u):
@@ -475,12 +454,7 @@
     ]
     for load in loads:
         load.start()
-    others = []
-    for r in range(side):
-        for c in range(side):
-            if r or c:
-                others.append({"row": lax.rem(p + r, side), "col": lax.rem(q + c, side)})
-    meet(others)
+    yield
 
     def masked(t, u):
         if packed:
@@ -489,7 +463,8 @@
 
     loads[0].wait()
     column[0] = column[0] * masked(0, 0)
-    gather_corner(group, column)
+    corner = Corner(group, column)
+    corner.open()
     for t in range(1, rows):
         loads[t].wait()
         column[t] = column[t] * masked(t, 0)
@@ -507,69 +482,81 @@
         for j in range(k):
             count = count + jnp.where(kind[j] == kind[k], 1, 0)
         rank.append(jnp.minimum(count, 1))
-    chosen = []
     for r in range(side):
-        pair = []
         for i in range(2):
             found = jnp.int32(0)
             for k in range(runs):
                 hit = jnp.logical_and(kind[k] == r, rank[k] == i)
                 found = jnp.where(hit, k, found)
-            pair.append(found)
-        chosen.append(pair)
-
-    def slots_of(r, c):
-        if r == c:
-            return [(0, 0), (1, 0), (1, 1)]
-        if 1 <= r < c:
-            return []
-        return [(0, 0), (0, 1), (1, 0), (1, 1)]
-
-    moves = []
-    for c in range(side):
-        for r in range(side):
-            slots = slots_of(r, c)
-            if not slots:
-                continue
-            for slot, (i, j) in enumerate(slots):
-                k, l = chosen[r][i], chosen[c][j]
+            table[r * 2 + i] = found
+
+    def fill(index, carry):
+        r, c = index // side, lax.rem(index, side)
+
+        @pl.when(jnp.logical_or(r == 0, jnp.logical_or(c == 0, r >= c)))
+        def _():
+            for slot in range(4):
+                k, l = table[r * 2 + slot % 2], table[c * 2 + slot // 2]
                 k, l = jnp.maximum(k, l), jnp.minimum(k, l)
                 block = inner[k * runs + l]
                 if not packed:
-                    block = block * mask_ref[side * (k + 1) + p, side * (l + 1) + q].astype(f32)
-                if r or c:
-                    pack[r * side + c, slot] = block
-                else:
-                    recv[0, slot] = block
-            if r or c:
-                moves.append((r, c, len(slots)))
-
-    def move(r, c, count):
+                    mark = mask_ref[side * (k + 1) + p, side * (l + 1) + q]
+                    block = block * mark.astype(f32)
+                pack[index, slot] = block
+
+        return carry
+
+    lax.fori_loop(0, side * side, fill, 0)
+    near[0] = pack[0, 0:2]
+    late[0] = pack[0]
+
+    moves = [
+        (r, c)
+        for c in range(side)
+        for r in range(side)
+        if (r or c) and (r == 0 or c == 0 or r >= c)
+    ]
+    ahead = [(r, c) for r, c in moves if c + 1 < side]
+
+    def send_near(r, c):
         index = r * side + c
-        return lambda: group.copy(
-            pack.at[index, 0:count],
-            recv.at[index, 0:count],
+        return group.copy(
+            pack.at[index, 0:2],
+            near.at[index],
+            n_send.at[index],
+            n_recv.at[index],
+            {"row": lax.rem(p + r, side), "col": lax.rem(q + c, side)},
+        )
+
+    def send_late(r, c):
+        index = r * side + c
+        first = 0 if c + 1 == side else 3 if r == c else 2
+        return group.copy(
+            pack.at[index, first:4],
+            late.at[index, first:4],
             f_send.at[index],
             f_recv.at[index],
             {"row": lax.rem(p + r, side), "col": lax.rem(q + c, side)},
         )
 
-    gather_strips(group)
-    load_corner(group, inverse)
-    order = sorted(moves, key=lambda m: -min(m[1], side - m[1]))
-    per = -(-len(order) // (side - 1))
+    early = [(r, c) for r, c in moves if c % 2 == 0]
+    other = [(r, c) for r, c in moves if c % 2]
+    ahead.sort(key=lambda m: -m[1])
 
     def extra(step):
-        for turn in range(side - 1):
-
-            @pl.when(step == turn)
-            def _():
-                for r, c, count in order[turn * per : (turn + 1) * per]:
-                    move(r, c, count)().start()
-
-    factor(group, lines, inverse, upper, row_ref, extra)
+        @pl.when(step == max(side - 3, 0))
+        def _():
+            for r, c in ahead:
+                send_near(r, c).start()
+
+        @pl.when(step == side - 2)
+        def _():
+            for r, c in early:
+                send_late(r, c).start()
+
+    corner.spread()
+    factor(group, corner, lines, (row_ref, upper, hi, lo), extra)
     lines.last()
-    inv_hi[...], inv_lo[...] = split(inverse[...])
 
     def home(spot, mine):
         row_k = row_ps = ok = kinds = ranks = jnp.int32(0)
@@ -590,25 +577,18 @@
         )
 
     def times(index, carry):
-        value = product(split(tall[index]), (inv_hi[...], inv_lo[...]))
+        value = product(split(tall[index]), (hi[...], lo[...]))
         at = pl.ds(pl.multiple_of(index * 2 * size, 2 * size), 2 * size)
         l_hi[at, :], l_lo[at, :] = split(value)
         return carry
 
-    lax.fori_loop(0, rows, times, 0)
-    own = pl.ds(pl.multiple_of(q * size, size), size)
-    panel_ref[0] = top_block(upper, p, q, size)
-    left = wide[p, 1:rows].reshape(runs * size, side * size)
-    below = product(split(left), (inv_hi[own, :], inv_lo[own, :]))
-    panel_ref[1:rows] = below.reshape(runs, size, size)
-
-    for r, c, count in order:
-        move(r, c, count)().wait()
+    count = (rows + 2) // 2
+    lax.fori_loop(0, count, times, 0)
     high = rows * size
     row_id = lax.broadcasted_iota(jnp.int32, (size, size), 0)
     col_id = lax.broadcasted_iota(jnp.int32, (size, size), 1)
-    ranges = [(0, 1)] + [(u, min(u + 2, rows)) for u in range(1, rows, 2)]
-    for first, end in ranges:
+
+    def build(first, end):
         taken = slice(first * size, high)
         given = slice(high + first * size, high + end * size)
         out = product((l_hi[taken, :], l_lo[taken, :]), (l_hi[given, :], l_lo[given, :]))
@@ -616,8 +596,12 @@
             _, _, c_ok, c_kind, c_rank = col_home[u]
             for t in range(u, rows):
                 _, _, r_ok, r_kind, r_rank = row_home[t]
-                slot = jnp.where(r_kind == c_kind, r_rank + c_rank, 2 * r_rank + c_rank)
-                block = recv[r_kind * side + c_kind, slot]
+                index = r_kind * side + c_kind
+                if u == 0:
+                    block = near[index, r_rank]
+                else:
+                    ready = jnp.logical_and(c_rank == 0, c_kind + 1 < side)
+                    block = jnp.where(ready, near[index, r_rank], late[index, 2 * c_rank + r_rank])
                 value = jnp.where(r_ok * c_ok > 0, block, 0.0)
                 value = value - out[
                     (t - first) * size : (t - first + 1) * size,
@@ -630,15 +614,49 @@
                     on = jnp.logical_and(row_id == col_id, p == q)
                     value = value + jnp.where(on, diag_ref[t] * factor_here, 0.0)
                 part_ref[tri(t, u, rows)] = value
+
+    def arrived(spot, send, receive):
+        group.copy(spot, spot, send, receive, {"row": p}).wait_recv()
+
+    for r, c in ahead:
+        index = r * side + c
+        arrived(near.at[index], n_send.at[0], n_recv.at[index])
+    build(0, 1)
+    yield
+
+    lax.fori_loop(count, rows, times, 0)
+    own = pl.ds(pl.multiple_of(q * size, size), size)
+    panel_ref[0] = top_block(upper, p, q, size)
+    left = wide[p, 1:rows].reshape(runs * size, side * size)
+    below = product(split(left), (hi[own, :], lo[own, :]))
+    panel_ref[1:rows] = below.reshape(runs, size, size)
+    yield
+
+    for r, c in other:
+        send_late(r, c).start()
+    yield
+
+    for r, c in moves:
+        index = r * side + c
+        first = 0 if c + 1 == side else 3 if r == c else 2
+        arrived(late.at[index, first:4], f_send.at[0], f_recv.at[index])
+    for first in range(1, rows, 2):
+        build(first, min(first + 2, rows))
+        yield
+    for r, c in moves:
+        send_late(r, c).wait_send()
+    for r, c in ahead:
+        send_near(r, c).wait_send()
+    corner.finish()
     lines.finish()
-    group.finish()
+    yield
 
 
 def params(name, key):
     return dict(
         name=name,
         compiler_params=pltpu.CompilerParams(
-            collective_id=key, has_side_effects=True, vmem_limit_bytes=60 * 2**20
+            collective_id=key, has_side_effects=True, vmem_limit_bytes=62 * 2**20
         ),
     )
 
@@ -646,18 +664,66 @@
 VM = pl.BlockSpec(memory_space=pltpu.VMEM)
 SM = pl.BlockSpec(memory_space=pltpu.SMEM)
 ANY = pl.BlockSpec(memory_space=pl.ANY)
-
-
-def run_child(key, packed, child, parent, maps, mask, above, front, share, diag, side):
-    rows, size = share.shape[0], share.shape[1]
+VMEM, DMA = pltpu.VMEM, pltpu.SemaphoreType.DMA
+
+
+def child_scratch(rows, size, side):
+    order = side * size
     runs = rows - 1
-    order = side * size
+    return [
+        VMEM((rows, size, size), f32),
+        VMEM((runs * runs, size, size), f32),
+        VMEM((side * side, 4, size, size), f32),
+        VMEM((side * side, 2, size, size), f32),
+        VMEM((side * side, 4, size, size), f32),
+        VMEM((side, rows, size, order), f32),
+        VMEM((size, order), f32),
+        VMEM((order, order), f32),
+        VMEM((order, order), bf16),
+        VMEM((order, order), bf16),
+        VMEM((rows, 2 * size, order), f32),
+        VMEM((2 * rows * size, order), bf16),
+        VMEM((2 * rows * size, order), bf16),
+        pltpu.SMEM((2 * side,), jnp.int32),
+    ], [
+        DMA((rows * (rows + 1) // 2,)),
+        DMA((side * side,)),
+        DMA((side * side,)),
+        DMA((side * side,)),
+        DMA((side * side,)),
+        *gather_sems(side),
+    ]
+
+
+def around(side):
+    p, q = lax.axis_index("row"), lax.axis_index("col")
+    return [
+        {"row": lax.rem(p + r, side), "col": lax.rem(q + c, side)}
+        for r in range(side)
+        for c in range(side)
+        if r or c
+    ]
+
+
+def run_child(key, packed, child, parent, inputs, side):
+    rows, size = inputs[4].shape[0], inputs[4].shape[1]
     lower = rows * (rows + 1) // 2
-    VMEM, DMA = pltpu.VMEM, pltpu.SemaphoreType.DMA
-
-    def body(*refs):
+    refs, sems = child_scratch(rows, size, side)
+
+    def body(*args):
+        panel_ref, part_ref = args[6:8]
+        mine = args[8 : 8 + len(refs)]
+        flags = args[8 + len(refs) :]
         leaf = lax.axis_index("leaf")
-        child_kernel(packed, (leaf // child, leaf // parent), *refs)
+        group = Group(side, rows, size, mine[5], flags[5:])
+        node = (leaf // child, leaf // parent)
+        phase = child_phase(
+            packed, node, args[:6], part_ref, panel_ref, mine, flags[:5], group
+        )
+        next(phase)
+        meet(around(side))
+        for _ in phase:
+            pass
 
     return pl.pallas_call(
         body,
@@ -667,69 +733,46 @@
         ),
         in_specs=[SM, SM, SM, ANY, VM, VM],
         out_specs=(VM, VM),
-        scratch_shapes=[
-            VMEM((rows, size, size), f32),
-            VMEM((runs * runs, size, size), f32),
-            VMEM((side * side, 4, size, size), f32),
-            VMEM((side * side, 4, size, size), f32),
-            VMEM((side, rows, size, order), f32),
-            VMEM((order, order), f32),
-            VMEM((order, order), f32),
-            VMEM((size, order), f32),
-            VMEM((order, order), bf16),
-            VMEM((order, order), bf16),
-            VMEM((rows, 2 * size, order), f32),
-            VMEM((2 * rows * size, order), bf16),
-            VMEM((2 * rows * size, order), bf16),
-            DMA((lower,)),
-            DMA((side * side,)),
-            DMA((side * side,)),
-            *gather_sems(side),
-        ],
+        scratch_shapes=refs + sems,
         **params(f"child_{key}", key),
-    )(maps, mask, above, front, share, diag)
-
-
-def top_kernel(
-    bit,
-    mine,
-    early,
-    panels_ref,
-    top_ref,
-    theirs,
-    column,
-    wide,
-    inverse,
-    upper,
-    row_ref,
-    inv_hi,
-    inv_lo,
-    l_hi,
-    l_lo,
-    done,
-    blank,
-    x_send,
-    x_recv,
-    out_sem,
-    *sems,
-):
+    )(*inputs)
+
+
+def top_kernel(packed, child, parent, bit, side, n_refs, *args):
+    front_refs, args = args[:6], args[6:]
+    panels_ref, top_ref = args[:2]
+    child_refs, args = args[2 : 2 + n_refs], args[2 + n_refs :]
+    mine, theirs, column, wide, l_hi, l_lo, done, blank, x_send, x_recv, out_sem = args[:11]
+    flags = args[11:]
+    child_sems, flags = flags[:5], flags[5:]
+    half = len(flags) // 2
     rows, size = column.shape[0], column.shape[1]
     runs = rows - 1
-    side = wide.shape[0]
-    group = Group(side, rows, size, wide, sems)
-    p, q = group.p, group.q
     leaf = lax.axis_index("leaf")
     partner = leaf + bit - 2 * bit * lax.rem(leaf // bit, 2)
-    places = [{"leaf": partner}, {"row": group.core}, {"row": group.far}]
-    for hop in range(1, side):
-        places.append({"col": lax.rem(q + hop, side)})
-    meet(places)
-    lower = mine.shape[0]
-    cuts = [(0, 1), (1, rows), (rows, lower)]
+    first_group = Group(side, rows, size, child_refs[5], flags[:half])
+    phase = child_phase(
+        packed,
+        (leaf // child, leaf // parent),
+        front_refs,
+        mine,
+        panels_ref.at[0],
+        child_refs,
+        child_sems,
+        first_group,
+    )
+    next(phase)
+    meet(around(side) + [{"leaf": partner}])
+    row_ref, upper, hi, lo = child_refs[6:10]
+    group = Group(side, rows, size, wide, flags[half:])
+    p, q = group.p, group.q
+    cuts = [(0, 1), (1, rows)]
+    for u in range(1, rows, 2):
+        cuts.append((cuts[-1][1], cuts[-1][1] + sum(rows - v for v in range(u, min(u + 2, rows)))))
 
     def trade(index):
         low, high = cuts[index]
-        return lambda: group.copy(
+        return group.copy(
             mine.at[low:high],
             theirs.at[low:high],
             x_send.at[index],
@@ -737,45 +780,11 @@
             {"leaf": partner},
         )
 
-    for index in range(len(cuts)):
-        group.start(True, trade(index))
+    next(phase)
+    trade(0).start()
+    trade(1).start()
+    next(phase)
     blank[...] = jnp.zeros_like(blank)
-    for k in range(panels_ref.shape[0] - 1):
-        panels_ref[k] = early[k]
-    trade(0)().wait_recv()
-    column[0] = mine[0] + theirs[0]
-    gather_corner(group, column)
-    trade(1)().wait_recv()
-    for t in range(1, rows):
-        column[t] = mine[t] + theirs[t]
-    wide[p, 1:rows, :, group.columns(q)] = column[1:rows]
-    lines = Lines(group, column, False)
-    lines.open()
-    gather_strips(group)
-    load_corner(group, inverse)
-    factor(group, lines, inverse, upper, row_ref, lambda step: None)
-    lines.last()
-    inv_hi[...], inv_lo[...] = split(inverse[...])
-    last = panels_ref.shape[0] - 1
-    panels_ref[last, 0] = top_block(upper, p, q, size)
-    own = pl.ds(pl.multiple_of(q * size, size), size)
-
-    def times(index, carry):
-        row = jnp.where(index < runs, p, q)
-        t = jnp.where(index < runs, index, index - runs) + 1
-        value = product(split(wide[row, t]), (inv_hi[...], inv_lo[...]))
-        at = pl.ds(pl.multiple_of(index * size, size), size)
-        l_hi[at, :], l_lo[at, :] = split(value)
-        return carry
-
-    lax.fori_loop(0, 2 * runs, times, 0)
-    left = wide[p, 1:rows].reshape(runs * size, side * size)
-    below = product(split(left), (inv_hi[own, :], inv_lo[own, :]))
-    panels_ref[last, 1:rows] = below.reshape(runs, size, size)
-    trade(2)().wait_recv()
-    high = runs * size
-    row_id = lax.broadcasted_iota(jnp.int32, (size, size), 0)
-    col_id = lax.broadcasted_iota(jnp.int32, (size, size), 1)
     writes = []
     for k in range(runs):
         for l in range(runs):
@@ -787,11 +796,53 @@
             )
             if k < l:
                 writes[-1].start()
+    trade(0).wait_recv()
+    column[0] = mine[0] + theirs[0]
+    corner = Corner(group, column)
+    corner.open()
+    corner.spread()
+    trade(1).wait_recv()
+    for t in range(1, rows):
+        column[t] = mine[t] + theirs[t]
+    wide[p, 1:rows, :, group.columns(q)] = column[1:rows]
+    lines = Lines(group, column, False)
+    lines.open()
+
+    def extra(step):
+        @pl.when(step == max(side - 3, 0))
+        def _():
+            next(phase)
+
+    factor(group, corner, lines, (row_ref, upper, hi, lo), extra)
+    for index in range(2, len(cuts)):
+        next(phase)
+        trade(index).start()
+    lines.last()
+    last = panels_ref.shape[0] - 1
+    panels_ref[last, 0] = top_block(upper, p, q, size)
+    own = pl.ds(pl.multiple_of(q * size, size), size)
+
+    def times(index, carry):
+        row = jnp.where(index < runs, p, q)
+        t = jnp.where(index < runs, index, index - runs) + 1
+        value = product(split(wide[row, t]), (hi[...], lo[...]))
+        at = pl.ds(pl.multiple_of(index * size, size), size)
+        l_hi[at, :], l_lo[at, :] = split(value)
+        return carry
+
+    lax.fori_loop(0, 2 * runs, times, 0)
+    left = wide[p, 1:rows].reshape(runs * size, side * size)
+    below = product(split(left), (hi[own, :], lo[own, :]))
+    panels_ref[last, 1:rows] = below.reshape(runs, size, size)
+    high = runs * size
+    row_id = lax.broadcasted_iota(jnp.int32, (size, size), 0)
+    col_id = lax.broadcasted_iota(jnp.int32, (size, size), 1)
     for first in range(0, runs, 2):
         end = min(first + 2, runs)
         taken = slice(first * size, high)
         given = slice(high + first * size, high + end * size)
         out = product((l_hi[taken, :], l_lo[taken, :]), (l_hi[given, :], l_lo[given, :]))
+        trade(2 + first // 2).wait_recv()
         for l in range(first, end):
             for k in range(l, runs):
                 at = tri(k + 1, l + 1, rows)
@@ -804,45 +855,48 @@
                     value = jnp.where(keep, value, 0.0)
                 done[k * runs + l] = value
                 writes[k * runs + l].start()
+    next(phase)
     for write in writes:
         write.wait()
+    for index in range(len(cuts)):
+        trade(index).wait_send()
+    corner.finish()
     lines.finish()
-    group.finish()
-
-
-def run_top(key, bit, part, early, rows, side):
-    size = part.shape[1]
+
+
+def run_top(key, packed, child, parent, bit, inputs, side):
+    rows, size = inputs[4].shape[0], inputs[4].shape[1]
     runs = rows - 1
     order = side * size
-    VMEM, DMA = pltpu.VMEM, pltpu.SemaphoreType.DMA
+    lower = rows * (rows + 1) // 2
+    refs, sems = child_scratch(rows, size, side)
+    cuts = 2 + -(-runs // 2)
     return pl.pallas_call(
-        functools.partial(top_kernel, bit),
+        functools.partial(top_kernel, packed, child, parent, bit, side, len(refs)),
         out_shape=(
-            jax.ShapeDtypeStruct((early.shape[0] + 1, rows, size, size), f32),
+            jax.ShapeDtypeStruct((2, rows, size, size), f32),
             jax.ShapeDtypeStruct((1, runs, 1, size, runs, 1, size), f32),
         ),
-        in_specs=[VM, VM],
+        in_specs=[SM, SM, SM, ANY, VM, VM],
         out_specs=(VM, ANY),
         scratch_shapes=[
-            VMEM(part.shape, f32),
+            *refs,
+            VMEM((lower, size, size), f32),
+            VMEM((lower, size, size), f32),
             VMEM((rows, size, size), f32),
             VMEM((side, rows, size, order), f32),
-            VMEM((order, order), f32),
-            VMEM((order, order), f32),
-            VMEM((size, order), f32),
-            VMEM((order, order), bf16),
-            VMEM((order, order), bf16),
             VMEM((2 * runs * size, order), bf16),
             VMEM((2 * runs * size, order), bf16),
             VMEM((runs * runs, size, size), f32),
             VMEM((size, size), f32),
-            DMA((3,)),
-            DMA((3,)),
+            DMA((cuts,)),
+            DMA((cuts,)),
             DMA((runs * runs,)),
+            *sems,
             *gather_sems(side),
         ],
         **params(f"top_{key}", key),
-    )(part, early)
+    )(*inputs)
 
 
 def partner_2(block, axis, bit):
@@ -865,30 +919,29 @@
     front, packed = leaf_front, False
     panel_list = []
     for depth in range(levels):
-        panel, part = run_child(
-            depth,
-            packed,
-            1 << depth,
-            2 << depth,
+        inputs = (
             ext_map[depth],
             leaf_pattern[0],
             parent_pattern[depth],
             front,
             share[depth],
             diag[depth],
-            side,
         )
-        panel_list.append(panel)
-        if depth + 1 < levels:
-            front = part + partner_2(part, "leaf", depth)
-            packed = True
-            higher = (share[depth + 1 :], diag[depth + 1 :])
-            other = partner_2(higher, "leaf", depth)
-            share = jnp.concatenate([share[: depth + 1], higher[0] + other[0]], axis=0)
-            diag = jnp.concatenate([diag[: depth + 1], higher[1] + other[1]], axis=0)
-    panels, top_update = run_top(
-        levels, 1 << (levels - 1), part, jnp.stack(panel_list), rows, side
-    )
+        if depth + 1 == levels:
+            panels, top_update = run_top(
+                depth, packed, 1 << depth, 2 << depth, 1 << depth, inputs, side
+            )
+            break
+        panel, part = run_child(depth, packed, 1 << depth, 2 << depth, inputs, side)
+        panel_list.append(panel[None])
+        front = part + partner_2(part, "leaf", depth)
+        packed = True
+        higher = (share[depth + 1 :], diag[depth + 1 :])
+        other = partner_2(higher, "leaf", depth)
+        share = jnp.concatenate([share[: depth + 1], higher[0] + other[0]], axis=0)
+        diag = jnp.concatenate([diag[: depth + 1], higher[1] + other[1]], axis=0)
+    if panel_list:
+        panels = jnp.concatenate(panel_list + [panels], axis=0)
     return (panels.reshape(levels + 1, 1, rows, 1, size, 1, size), top_update)
 
 

time: 219 us -> 187 us (0.85)
  the two profiles are of different devices: /device:TPU:0 before, /device:TPU:4 now
where the time goes in v1:
time: 187 us
  Pallas kernels  177 us (95%)
  local copies, waits for them, and re-layouts  9.55 us (5%)
    pallas_call x1, Pallas kernels, run_top(): pl.pallas_call(functools.partial(top_kernel, packed, child, parent, bit,...  177 us
    unnamed x4, local copies, waits for them, and re-layouts  9.55 us

profile of v1, /device:TPU:4, one launch (start us, length us, event | category | flops | bytes accessed | tf_op | source)
XLA Modules:
  0.0 186.9 jit_solution(10746210620966502321)
XLA Ops:
  0.6 1.3 copy.14
  1.9 1.4 copy.13
  3.3 176.7 %top_0.1 = (f32[2,7,128,128]{3,2,1,0:T(8,128)}, f32[1,6,1,128,6,1,128]{6,5,4,3,2,1,0:T(1,128)}) custom-call(s32[2,24]{1,0:T(2,128)} %bitcast.17, s32[28,28]{1,0:T(8,128)} %bitcast.15, s32[2,28,28]{2,1,0:T(8,128)} %bitcast.14, f32[1,7,1,128,7,1,128]{6,5,4,3,2,1,0:T(1,128)} %args_3_.4, f32[7,128,128]{2,1,0:T(8,128)} %bitcast.13, f32[7,1,128]{2,1,0:T(1,128)} %bitcast.16), custom_call_target="tpu_custom_call" | custom-call | tf_op jit(solution)/shard_map/top_0/pallas_call | solution.py:874
  180.1 2.2 %copy.17 = f32[2,1,7,1,128,1,128]{6,5,4,3,2,1,0:T(1,128)} copy(f32[2,1,7,1,128,1,128]{6,5,4,3,2,1,0:T(1,128)} %bitcast.12) | data formatting | bytes 1835008
  182.2 4.7 %copy.18 = f32[1,6,1,128,6,1,128]{6,5,4,3,2,1,0:T(1,128)} copy(f32[1,6,1,128,6,1,128]{6,5,4,3,2,1,0:T(1,128)} %get-tuple-element.11) | data formatting | bytes 4718592

commit v2 on v1

--- a/solution.py
+++ b/solution.py
@@ -331,6 +331,7 @@
     def last(self):
         g = self.group
         send, receive = g.sems[6:8]
+        self.pass_on(g.side - 1, begin, True)
         for index, row in ((1, g.core), (2, g.diagonal)):
             for source in range(g.side):
 
@@ -347,7 +348,6 @@
                 run(self.wanted(row), wait)
 
     def open(self):
-        self.hop(1, begin)
         self.across(0, begin)
 
     def advance(self, step):
@@ -363,7 +363,8 @@
 
             self.across(step + 1, begin)
 
-        self.pass_on(step, begin, True)
+    def lag(self, step):
+        pl.when(step > 0)(lambda: self.pass_on(step - 1, begin, True))
 
     def finish(self):
         def body(step, carry):
@@ -424,6 +425,7 @@
         pivot_step(step, group.size, corner.row, work)
         lines.advance(step)
         extra(step)
+        lines.lag(step)
         return carry
 
     lax.fori_loop(0, group.side, body, 0)
@@ -459,7 +461,7 @@
     def masked(t, u):
         if packed:
             return 1.0
-        return mask_ref[side * t + p, side * u + q].astype(f32)
+        return mask_ref[side * t + p, 0, side * u + q].astype(f32)
 
     loads[0].wait()
     column[0] = column[0] * masked(0, 0)
@@ -470,7 +472,7 @@
         column[t] = column[t] * masked(t, 0)
     wide[p, 1:rows, :, group.columns(q)] = column[1:rows]
     lines = Lines(group, column, True)
-    lines.open()
+    lines.hop(1, begin)
     for index in range(rows, len(spots)):
         loads[index].wait()
 
@@ -500,7 +502,7 @@
                 k, l = jnp.maximum(k, l), jnp.minimum(k, l)
                 block = inner[k * runs + l]
                 if not packed:
-                    mark = mask_ref[side * (k + 1) + p, side * (l + 1) + q]
+                    mark = mask_ref[side * (k + 1) + p, 0, side * (l + 1) + q]
                     block = block * mark.astype(f32)
                 pack[index, slot] = block
 
@@ -555,6 +557,7 @@
                 send_late(r, c).start()
 
     corner.spread()
+    lines.open()
     factor(group, corner, lines, (row_ref, upper, hi, lo), extra)
     lines.last()
 
@@ -608,9 +611,9 @@
                     (u - first) * size : (u - first + 1) * size,
                 ]
                 if u == 0:
-                    value = value + share_ref[t] * above_ref[parent, side * t + p, q].astype(f32)
+                    value = value + share_ref[t] * above_ref[side * t + p, parent, q].astype(f32)
                 if t == u:
-                    factor_here = above_ref[parent, side * t + p, side * t + q].astype(f32)
+                    factor_here = above_ref[side * t + p, parent, side * t + q].astype(f32)
                     on = jnp.logical_and(row_id == col_id, p == q)
                     value = value + jnp.where(on, diag_ref[t] * factor_here, 0.0)
                 part_ref[tri(t, u, rows)] = value
@@ -806,6 +809,7 @@
         column[t] = mine[t] + theirs[t]
     wide[p, 1:rows, :, group.columns(q)] = column[1:rows]
     lines = Lines(group, column, False)
+    lines.hop(1, begin)
     lines.open()
 
     def extra(step):
@@ -822,15 +826,19 @@
     panels_ref[last, 0] = top_block(upper, p, q, size)
     own = pl.ds(pl.multiple_of(q * size, size), size)
 
+    pair = 2 - runs % 2
+    turns = runs // pair
+
     def times(index, carry):
-        row = jnp.where(index < runs, p, q)
-        t = jnp.where(index < runs, index, index - runs) + 1
-        value = product(split(wide[row, t]), (hi[...], lo[...]))
-        at = pl.ds(pl.multiple_of(index * size, size), size)
+        row = jnp.where(index < turns, p, q)
+        t = jnp.where(index < turns, index, index - turns) * pair + 1
+        blocks = wide[row, pl.ds(t, pair)].reshape(pair * size, side * size)
+        value = product(split(blocks), (hi[...], lo[...]))
+        at = pl.ds(pl.multiple_of(index * pair * size, pair * size), pair * size)
         l_hi[at, :], l_lo[at, :] = split(value)
         return carry
 
-    lax.fori_loop(0, 2 * runs, times, 0)
+    lax.fori_loop(0, 2 * turns, times, 0)
     left = wide[p, 1:rows].reshape(runs * size, side * size)
     below = product(split(left), (hi[own, :], lo[own, :]))
     panels_ref[last, 1:rows] = below.reshape(runs, size, size)
@@ -921,8 +929,8 @@
     for depth in range(levels):
         inputs = (
             ext_map[depth],
-            leaf_pattern[0],
-            parent_pattern[depth],
+            leaf_pattern.transpose(1, 0, 2),
+            parent_pattern[depth].transpose(1, 0, 2),
             front,
             share[depth],
             diag[depth],

time: 187 us -> 185 us (0.989)
  the two profiles are of different devices: /device:TPU:4 before, /device:TPU:0 now
where the time goes in v2:
time: 185 us; the launch traced here: 184 us
  Pallas kernels  177 us (96%)
  local copies, waits for them, and re-layouts  6.86 us (4%)
    pallas_call x1, Pallas kernels, run_top(): pl.pallas_call(functools.partial(top_kernel, packed, child, parent, bit,...  177 us
    unnamed x2, local copies, waits for them, and re-layouts  6.86 us

profile of v2, /device:TPU:0, one launch (start us, length us, event | category | flops | bytes accessed | tf_op | source)
XLA Modules:
  0.0 184.4 jit_solution(14313809749675582541)
XLA Ops:
  0.6 176.9 %top_0.1 = (f32[2,7,128,128]{3,2,1,0:T(8,128)}, f32[1,6,1,128,6,1,128]{6,5,4,3,2,1,0:T(1,128)}) custom-call(s32[2,24]{1,0:T(2,128)} %bitcast.15, s32[28,1,28]{2,1,0:T(1,128)} %bitcast.13, s32[28,2,28]{2,1,0:T(2,128)} %bitcast.12, f32[1,7,1,128,7,1,128]{6,5,4,3,2,1,0:T(1,128)} %args_3_.4, f32[7,128,128]{2,1,0:T(8,128)} %bitcast.11, f32[7,1,128]{2,1,0:T(1,128)} %bitcast.14), custom_call_target="tpu_custom_call" | custom-call | tf_op jit(solution)/shard_map/top_0/pallas_call | solution.py:882
  177.5 2.2 %copy.11 = f32[2,1,7,1,128,1,128]{6,5,4,3,2,1,0:T(1,128)} copy(f32[2,1,7,1,128,1,128]{6,5,4,3,2,1,0:T(1,128)} %bitcast.10) | data formatting | bytes 1835008
  179.7 4.7 %copy.12 = f32[1,6,1,128,6,1,128]{6,5,4,3,2,1,0:T(1,128)} copy(f32[1,6,1,128,6,1,128]{6,5,4,3,2,1,0:T(1,128)} %get-tuple-element.11) | data formatting | bytes 4718592
